TPU v7x, 32 devices: a whole 2x2x4 slice. The times are simulated.
32 devices in a mesh: tm: 16 (over z, x, core), rows: 2 (over y).
Axes of the slice: x: 2, y: 2, z: 4, core: 2. Of those that a mesh axis runs over, the one named last changes fastest.
Arguments:
- video: bfloat16 [32, 16, 480, 128], P('tm', 'rows'), may hold values from -1000 to 1000, as said below
- spatial_weight: bfloat16 [3, 3, 128, 128], replicated, may hold values from -0.1875 to 0.1875
- norm_gain: float32 [128], replicated, may hold values from 0.5 to 1.5
- norm_shift: float32 [128], replicated, may hold values from -3 to 3
- temporal_weight: bfloat16 [3, 3, 128, 128], replicated, may hold values from -0.3125 to 0.3125
Outputs:
- encoded: bfloat16 [32, 16, 480, 128], P('tm', 'rows')
Inputs may be any that keep to these rules, and one draw needn't show every extreme that they name: `video`: feature values are finite and of moderate size.
All inputs are finite; a program needn't handle non-finite values.
Results may differ from a plain program's by a relative error of at most 0.0065.
Values may be sent and summed in bfloat16 or wider, within the bound.
No kernel may reach another device: no remote copies, remote signals or barrier semaphores. Data moves between devices by JAX's collectives and lax.ppermute only.
A program may use at most 64 MiB of HBM per device.

v0:
```python
import jax
import jax.numpy as jnp
from jax import lax
from jax.sharding import PartitionSpec as P

GROUPS = 32


def padded_2(array, sides, width):
    for axis, dim in sides:
        size, length = (lax.axis_size(axis), array.shape[dim])
        up = [(i, (i + 1) % size) for i in range(size - 1)]
        down = [(j, i) for i, j in up]
        last = lax.slice_in_dim(array, length - width, length, axis=dim)
        leading = lax.slice_in_dim(array, 0, width, axis=dim)
        before = lax.ppermute(last, axis, up)
        after = lax.ppermute(leading, axis, down)
        array = jnp.concatenate([before, array, after], axis=dim)
    return array


def temporal_layer(extended, lead, dilation, kernels):
    own = extended.shape[0] - lead
    total = extended[lead:].astype(jnp.float32)
    for tap_index in range(3):
        start = lead - tap_index * dilation
        total = total + jnp.einsum(
            "trwc,cd->trwd",
            extended[start : start + own],
            kernels[tap_index],
            preferred_element_type=jnp.float32,
        )
    return total.astype(jnp.bfloat16)


def body(video, spatial_weight, norm_gain, norm_shift, temporal_weight):
    fr_local, band, width, chans = video.shape
    padded = padded_2(video, (("rows", 1),), 1)
    padded = jnp.pad(padded, ((0, 0), (0, 0), (1, 1), (0, 0)))
    pieces = [
        padded[:, row_tap : row_tap + band, col_tap : col_tap + width, :]
        for row_tap in range(3)
        for col_tap in range(3)
    ]
    patches = jnp.concatenate(pieces, axis=-1).reshape(fr_local * band * width, 9 * chans)
    conv = jnp.dot(
        patches, spatial_weight.reshape(9 * chans, chans), preferred_element_type=jnp.float32
    )
    per_group = chans // GROUPS
    grouped = conv.reshape(fr_local, band, width, GROUPS, per_group)
    part_sum = jnp.sum(grouped, axis=(1, 2, 4))
    part_square = jnp.sum(grouped * grouped, axis=(1, 2, 4))
    total_sum, total_square = lax.psum((part_sum, part_square), "rows")
    count = jnp.float32(band * lax.axis_size("rows") * width * per_group)
    mean = total_sum / count
    var = total_square / count - mean * mean
    normed = (grouped - mean[:, None, None, :, None]) * lax.rsqrt(var + 1e-05)[
        :, None, None, :, None
    ]
    normed = normed.reshape(fr_local, band, width, chans) * norm_gain + norm_shift
    hidden = jax.nn.silu(normed).astype(jnp.bfloat16)
    current = lax.all_to_all(hidden, "tm", split_axis=2, concat_axis=0, tiled=True)
    for layer, dilation in enumerate((1, 2, 4)):
        lead = 2 * dilation
        extended = jnp.pad(current, ((lead, 0), (0, 0), (0, 0), (0, 0)))
        current = temporal_layer(extended, lead, dilation, temporal_weight[layer])
    return lax.all_to_all(current, "tm", split_axis=0, concat_axis=2, tiled=True)


def solution(mesh):
    return jax.shard_map(
        body,
        mesh=mesh,
        in_specs=(P("tm", "rows", None, None), P(), P(), P(), P()),
        out_specs=P("tm", "rows", None, None),
        check_vma=False,
    )
```

profile of v0, /device:TPU:1, one launch (start us, length us, event | category | flops | bytes accessed | tf_op | source)
XLA Modules:
  0.0 154.6 jit_solution(4578269416225532073)
XLA Ops:
  0.0 1.1 fusion.36
  1.1 4.0 %collective-permute-start = (bf16[2,1,480,128]{3,2,1,0:T(8,128)(2,1)S(1)}, bf16[2,1,480,128]{3,2,1,0:T(8,128)(2,1)S(1)}, u32[]{:S(2)}, u32[]{:S(2)}) collective-permute-start(bf16[2,1,480,128]{3,2,1,0:T(8,128)(2,1)S(1)} %get-tuple-element.9), channel_id=1, source_target_pairs={{0,1},{2,3},{4,5},{6,7},{8,9},{10,11},{12,13},{14,15},{16,17},{18,... | collective-permute-start | bytes 737288 | tf_op jit(solution)/shard_map/ppermute | solution.py:16
  5.1 1.3 collective-permute-start.1
  6.4 1.2 copy.14
  7.6 0.1 dot_general.35
  7.6 0.0 copy-start
  7.7 2.0 %collective-permute-done = bf16[2,1,480,128]{3,2,1,0:T(8,128)(2,1)S(1)} collective-permute-done((bf16[2,1,480,128]{3,2,1,0:T(8,128)(2,1)S(1)}, bf16[2,1,480,128]{3,2,1,0:T(8,128)(2,1)S(1)}, u32[]{:S(2)}, u32[]{:S(2)}) %collective-permute-start) | collective-permute-done | bytes 245792 | tf_op jit(solution)/shard_map/ppermute | solution.py:16
  9.7 3.8 %collective-permute-done.1 = bf16[2,1,480,128]{3,2,1,0:T(8,128)(2,1)S(1)} collective-permute-done((bf16[2,1,480,128]{3,2,1,0:T(8,128)(2,1)S(1)}, bf16[2,1,480,128]{3,2,1,0:T(8,128)(2,1)S(1)}, u32[]{:S(2)}, u32[]{:S(2)}) %collective-permute-start.1) | collective-permute-done | bytes 245792 | tf_op jit(solution)/shard_map/ppermute | solution.py:17
  13.5 2.1 %fusion.7 = bf16[2,10,482,128]{3,2,1,0:T(8,128)(2,1)S(1)} fusion(bf16[2,1,480,128]{3,2,1,0:T(8,128)(2,1)S(1)} %collective-permute-done.1, bf16[2,8,480,128]{3,2,1,0:T(8,128)(2,1)} %param.5, bf16[2,1,480,128]{3,2,1,0:T(8,128)(2,1)S(1)} %collective-permute-done), kind=kLoop, calls=%fused_computation.15 | loop fusion | flops 14807040 | bytes 4925440 | tf_op jit(solution)/shard_map/concatenate | solution.py:18
  15.6 0.3 slice_dynamic-update-slice_fusion.5
  15.9 0.0 copy-done
  15.9 0.5 fusion.9
  16.4 0.8 slice_dynamic-update-slice_fusion.4
  17.2 0.5 slice_dynamic-update-slice_fusion.3
  17.7 0.5 constant_dynamic-update-slice_fusion
  18.2 0.8 slice_dynamic-update-slice_fusion.2
  19.0 0.5 slice_dynamic-update-slice_fusion.1
  19.5 0.5 fusion.8
  20.0 0.8 slice_dynamic-update-slice_fusion
  20.8 7.1 %fusion.35 = (f32[2,32]{1,0:T(2,128)S(1)}, f32[2,32]{1,0:T(2,128)S(1)}, f32[2,8,480,32,4]{2,3,4,1,0:T(8,128)}) fusion(bf16[32,4,1152,1,1]{2,1,0,4,3:T(4,128)(2,1)S(1)} %bitcast.100, bf16[2,8,480,1152]{3,2,1,0:T(8,128)(2,1)S(1)} %slice_dynamic-update-slice_fusion), kind=kOutput, calls=%fused_computation.54 | convolution fusion | flops 2267873280 | bytes 21922304 | tf_op jit(solution)/shard_map/dot_general | solution.py:46
  27.9 3.9 %all-reduce.4 = (f32[2,32]{1,0:T(2,128)S(1)}, f32[2,32]{1,0:T(2,128)S(1)}) all-reduce(f32[2,32]{1,0:T(2,128)S(1)} %get-tuple-element.6, f32[2,32]{1,0:T(2,128)S(1)} %get-tuple-element.5), channel_id=1, replica_groups=mesh['tm'=16,'rows'=2] {'rows'}, use_global_device_ids=true, to_apply=%region_3.4 | all-reduce | flops 128 | bytes 1024 | tf_op jit(solution)/shard_map/psum | solution.py:53
  31.8 2.9 %subtract_multiply_fusion = f32[2,8,480,32,4]{2,3,4,1,0:T(8,128)S(1)} fusion(f32[2,8,480,32,4]{2,3,4,1,0:T(8,128)} %get-tuple-element.13, f32[2,32]{1,0:T(2,128)S(1)} %get-tuple-element.12, f32[2,32]{1,0:T(2,128)S(1)} %get-tuple-element.11), kind=kLoop, calls=%fused_computation.7 | loop fusion | flops 1966080 | bytes 7864832 | tf_op jit(solution)/shard_map/mul | solution.py:57
  34.7 0.0 copy-start.2
  34.7 0.0 copy-start.3
  34.7 2.4 %copy.16 = f32[2,8,480,32,4]{2,1,4,3,0:T(8,128)S(1)} copy(f32[2,8,480,32,4]{2,3,4,1,0:T(8,128)S(1)} %subtract_multiply_fusion) | data formatting | bytes 7864320 | tf_op jit(solution)/shard_map/mul | solution.py:57
  37.2 0.0 copy-done.2
  37.2 0.0 copy-done.3
  37.2 1.4 multiply_convert_fusion
  38.7 3.4 %copy.17 = bf16[2,8,480,128]{3,1,0,2:T(8,128)(2,1)} copy(bf16[2,8,480,128]{2,1,3,0:T(8,128)(2,1)S(1)} %multiply_convert_fusion) | data formatting | bytes 3932160 | tf_op jit(solution)/shard_map/convert_element_type | solution.py:61
  42.0 0.0 copy-start.1
  42.0 54.3 %all_to_all.36 = bf16[2,8,480,128]{3,1,0,2:T(8,128)(2,1)S(1)} all-to-all(bf16[2,8,480,128]{3,1,0,2:T(8,128)(2,1)} %copy.17), channel_id=1, replica_groups=mesh['tm'=16,'rows'=2] {'tm'}, dimensions={2} | all-to-all | bytes 3932160 | tf_op jit(solution)/shard_map/all_to_all | solution.py:62
  96.4 0.3 copy.19
  96.7 0.0 copy-done.1
  96.7 0.7 fusion.22
  97.4 0.7 fusion.24
  98.0 0.9 add_convert_fusion.2
  99.0 0.6 fusion.17
  99.6 0.7 fusion.19
  100.3 1.0 add_convert_fusion.1
  101.3 0.7 fusion.12
  102.0 0.7 fusion.14
  102.6 1.0 add_convert_fusion
  103.6 49.4 %all_to_all.37 = bf16[32,8,30,128]{3,1,2,0:T(8,128)(2,1)S(1)} all-to-all(bf16[32,8,30,128]{3,1,2,0:T(8,128)(2,1)S(1)} %add_convert_fusion), channel_id=1, replica_groups=mesh['tm'=16,'rows'=2] {'tm'}, dimensions={0} | all-to-all | bytes 3932160 | tf_op jit(solution)/shard_map/all_to_all | solution.py:67
  153.0 0.1 copy.20
  153.1 1.5 copy.21
  (1 shorter events, 0.0 us)
Async XLA Ops:
  1.1 8.6 %collective-permute-start = (bf16[2,1,480,128]{3,2,1,0:T(8,128)(2,1)S(1)}, bf16[2,1,480,128]{3,2,1,0:T(8,128)(2,1)S(1)}, u32[]{:S(2)}, u32[]{:S(2)}) collective-permute-start(bf16[2,1,480,128]{3,2,1,0:T(8,128)(2,1)S(1)} %get-tuple-element.9), channel_id=1, source_target_pairs={{0,1},{2,3},{4,5},{6,7},{8,9},{10,11},{12,13},{14,15},{16,17},{18,... | collective-permute-start | bytes 737288 | tf_op jit(solution)/shard_map/ppermute | solution.py:16
  5.1 8.4 %collective-permute-start.1 = (bf16[2,1,480,128]{3,2,1,0:T(8,128)(2,1)S(1)}, bf16[2,1,480,128]{3,2,1,0:T(8,128)(2,1)S(1)}, u32[]{:S(2)}, u32[]{:S(2)}) collective-permute-start(bf16[2,1,480,128]{3,2,1,0:T(8,128)(2,1)S(1)} %get-tuple-element.10), channel_id=1, source_target_pairs={{1,0},{3,2},{5,4},{7,6},{9,8},{11,10},{13,12},{15,14},{17,16},{19,... | collective-permute-start | bytes 737288 | tf_op jit(solution)/shard_map/ppermute | solution.py:17
  7.6 8.3 %copy-start = (bf16[2,8,480,128]{3,2,1,0:T(8,128)(2,1)S(1)}, bf16[2,8,480,128]{3,2,1,0:T(8,128)(2,1)}, u32[]{:S(2)}) copy-start(bf16[2,8,480,128]{3,2,1,0:T(8,128)(2,1)} %param.5) | copy-start | bytes 5898244
  34.7 2.5 %copy-start.2 = (f32[128]{0:T(128)S(1)}, f32[128]{0:T(128)}, u32[]{:S(2)}) copy-start(f32[128]{0:T(128)} %param.8) | copy-start | bytes 1540
  34.7 2.5 %copy-start.3 = (f32[128]{0:T(128)S(1)}, f32[128]{0:T(128)}, u32[]{:S(2)}) copy-start(f32[128]{0:T(128)} %param.7) | copy-start | bytes 1540
  42.0 54.7 %copy-start.1 = (bf16[3,3,128,128]{3,2,1,0:T(8,128)(2,1)S(1)}, bf16[3,3,128,128]{3,2,1,0:T(8,128)(2,1)}, u32[]{:S(2)}) copy-start(bf16[3,3,128,128]{3,2,1,0:T(8,128)(2,1)} %param.9) | copy-start | bytes 884740
where the time goes:
time: 155 us
  blocking collectives  108 us (70%)
  local copies, waits for them, and re-layouts  14.3 us (9%)
  matrix products  13.9 us (9%)
  other arithmetic  7.38 us (5%)
  waiting for transfers between devices  5.84 us (4%)
  starting transfers between devices  5.28 us (3%)
    all_to_all x1, blocking collectives, body(): lax.all_to_all(hidden, 'tm', split_axis=2, concat_axis=0, tiled=True)  54.3 us
    all_to_all x1, blocking collectives, body(): lax.all_to_all(current, 'tm', split_axis=0, concat_axis=2, tiled=True)  49.4 us
    dot_general x1, matrix products, body(): jnp.dot(patches, spatial_weight.reshape(9 * chans, chans), preferred_elem...  7.06 us
    dot_general x9, matrix products, temporal_layer(): jnp.einsum('trwc,cd->trwd', extended[start:start + own], kernels[tap_inde...  6.82 us
    ppermute x1, starting transfers between devices, padded_2(): before = lax.ppermute(last, axis, up)  3.99 us
    psum x1, blocking collectives, body(): total_sum, total_square = lax.psum((part_sum, part_square), 'rows')  3.95 us
    ppermute x1, waiting for transfers between devices, padded_2(): after = lax.ppermute(leading, axis, down)  3.81 us
    unnamed x14, local copies, waits for them, and re-layouts  3.41 us
  transfers between devices with their start and end apart: 2, of which 2 were waited for; matrix products, arithmetic and copies ran while one was open for 1% of the time, Pallas kernels for 0%

commit v1 on v0

--- a/solution.py
+++ b/solution.py
@@ -59,7 +59,9 @@
     ]
     normed = normed.reshape(fr_local, band, width, chans) * norm_gain + norm_shift
     hidden = jax.nn.silu(normed).astype(jnp.bfloat16)
-    current = lax.all_to_all(hidden, "tm", split_axis=2, concat_axis=0, tiled=True)
+    parts = jnp.split(hidden, lax.axis_size("tm"), axis=2)
+    received = lax.all_to_all(jnp.stack(parts), "tm", 0, 0)
+    current = jnp.concatenate(received, axis=0)
     for layer, dilation in enumerate((1, 2, 4)):
         lead = 2 * dilation
         extended = jnp.pad(current, ((lead, 0), (0, 0), (0, 0), (0, 0)))

time: 155 us -> 191 us (1.23)
  local copies, waits for them, and re-layouts: 14.3 us -> 50.8 us
    another operation x0 -> x18, local copies, waits for them, and re-layouts: none -> 31.6 us  [body(): received = lax.all_to_all(jnp.stack(parts), 'tm', 0, 0)]
    unnamed x14 -> x39, local copies, waits for them, and re-layouts: 3.41 us -> 11.8 us
    convert_element_type x1 -> x0, local copies, waits for them, and re-layouts: 3.36 us -> none  [body(): hidden = jax.nn.silu(normed).astype(jnp.bfloat16)]
where the time goes in v1:
time: 191 us; the launch traced here: 190 us
  blocking collectives  107 us (56%)
  local copies, waits for them, and re-layouts  50.8 us (27%)
  matrix products  14 us (7%)
  other arithmetic  6.14 us (3%)
  waiting for transfers between devices  5.85 us (3%)
  starting transfers between devices  5.28 us (3%)
    all_to_all x1, blocking collectives, body(): received = lax.all_to_all(jnp.stack(parts), 'tm', 0, 0)  54 us
    all_to_all x1, blocking collectives, body(): lax.all_to_all(current, 'tm', split_axis=0, concat_axis=2, tiled=True)  49.4 us
    another operation x18, local copies, waits for them, and re-layouts, body(): received = lax.all_to_all(jnp.stack(parts), 'tm', 0, 0)  31.6 us
    unnamed x39, local copies, waits for them, and re-layouts  11.8 us
    dot_general x1, matrix products, body(): jnp.dot(patches, spatial_weight.reshape(9 * chans, chans), preferred_elem...  7.07 us
    dot_general x9, matrix products, temporal_layer(): jnp.einsum('trwc,cd->trwd', extended[start:start + own], kernels[tap_inde...  6.92 us
    ppermute x1, starting transfers between devices, padded_2(): before = lax.ppermute(last, axis, up)  3.99 us
    psum x1, blocking collectives, body(): total_sum, total_square = lax.psum((part_sum, part_square), 'rows')  3.95 us
  transfers between devices with their start and end apart: 2, of which 2 were waited for; matrix products, arithmetic and copies ran while one was open for 1% of the time, Pallas kernels for 0%

profile of v1, /device:TPU:1, one launch (start us, length us, event | category | flops | bytes accessed | tf_op | source)
XLA Modules:
  0.0 189.8 jit_solution(1694492770635463129)
XLA Ops:
  0.0 1.2 fusion.36
  1.2 4.0 %collective-permute-start = (bf16[2,1,480,128]{3,2,1,0:T(8,128)(2,1)S(1)}, bf16[2,1,480,128]{3,2,1,0:T(8,128)(2,1)S(1)}, u32[]{:S(2)}, u32[]{:S(2)}) collective-permute-start(bf16[2,1,480,128]{3,2,1,0:T(8,128)(2,1)S(1)} %get-tuple-element.25), channel_id=1, source_target_pairs={{0,1},{2,3},{4,5},{6,7},{8,9},{10,11},{12,13},{14,15},{16,17},{18,... | collective-permute-start | bytes 737288 | tf_op jit(solution)/shard_map/ppermute | solution.py:16
  5.2 1.3 collective-permute-start.1
  6.5 1.2 copy.13
  7.8 2.0 %collective-permute-done = bf16[2,1,480,128]{3,2,1,0:T(8,128)(2,1)S(1)} collective-permute-done((bf16[2,1,480,128]{3,2,1,0:T(8,128)(2,1)S(1)}, bf16[2,1,480,128]{3,2,1,0:T(8,128)(2,1)S(1)}, u32[]{:S(2)}, u32[]{:S(2)}) %collective-permute-start) | collective-permute-done | bytes 245792 | tf_op jit(solution)/shard_map/ppermute | solution.py:16
  9.8 3.8 %collective-permute-done.1 = bf16[2,1,480,128]{3,2,1,0:T(8,128)(2,1)S(1)} collective-permute-done((bf16[2,1,480,128]{3,2,1,0:T(8,128)(2,1)S(1)}, bf16[2,1,480,128]{3,2,1,0:T(8,128)(2,1)S(1)}, u32[]{:S(2)}, u32[]{:S(2)}) %collective-permute-start.1) | collective-permute-done | bytes 245792 | tf_op jit(solution)/shard_map/ppermute | solution.py:17
  13.6 0.9 fusion.7
  15.3 0.8 slice_dynamic-update-slice_fusion.4
  17.1 0.8 slice_dynamic-update-slice_fusion.2
  18.9 0.8 slice_dynamic-update-slice_fusion
  19.7 7.1 %fusion.35 = (f32[2,32]{1,0:T(2,128)S(1)}, f32[2,32]{1,0:T(2,128)S(1)}, f32[2,8,480,32,4]{2,3,4,1,0:T(8,128)}) fusion(bf16[32,4,1152,1,1]{2,1,0,4,3:T(4,128)(2,1)S(1)} %bitcast.128, bf16[2,8,480,1152]{3,2,1,0:T(8,128)(2,1)S(1)} %slice_dynamic-update-slice_fusion), kind=kOutput, calls=%fused_computation.86 | convolution fusion | flops 2267873280 | bytes 21922304 | tf_op jit(solution)/shard_map/dot_general | solution.py:46
  26.8 3.9 %all-reduce.4 = (f32[2,32]{1,0:T(2,128)S(1)}, f32[2,32]{1,0:T(2,128)S(1)}) all-reduce(f32[2,32]{1,0:T(2,128)S(1)} %get-tuple-element.6, f32[2,32]{1,0:T(2,128)S(1)} %get-tuple-element.5), channel_id=1, replica_groups=mesh['tm'=16,'rows'=2] {'rows'}, use_global_device_ids=true, to_apply=%region_3.4 | all-reduce | flops 128 | bytes 1024 | tf_op jit(solution)/shard_map/psum | solution.py:53
  30.7 2.9 %subtract_multiply_fusion = f32[2,8,480,32,4]{2,3,4,1,0:T(8,128)S(1)} fusion(f32[2,8,480,32,4]{2,3,4,1,0:T(8,128)} %get-tuple-element.29, f32[2,32]{1,0:T(2,128)S(1)} %get-tuple-element.28, f32[2,32]{1,0:T(2,128)S(1)} %get-tuple-element.27), kind=kLoop, calls=%fused_computation.7 | loop fusion | flops 1966080 | bytes 7864832 | tf_op jit(solution)/shard_map/mul | solution.py:57
  33.7 2.4 %copy.15 = f32[2,8,480,32,4]{2,1,4,3,0:T(8,128)S(1)} copy(f32[2,8,480,32,4]{2,3,4,1,0:T(8,128)S(1)} %subtract_multiply_fusion) | data formatting | bytes 7864320 | tf_op jit(solution)/shard_map/mul | solution.py:57
  36.1 1.4 multiply_convert_fusion
  37.6 4.1 %slice_bitcast_fusion = (bf16[1,2,8,30,128]{3,2,4,1,0:T(8,128)(2,1)S(1)}, bf16[1,2,8,30,128]{3,2,4,1,0:T(8,128)(2,1)S(1)}, bf16[1,2,8,30,128]{3,2,4,1,0:T(8,128)...) fusion(bf16[2,8,480,128]{2,1,3,0:T(8,128)(2,1)S(1)} %multiply_c, ...), kind=kLoop, calls=%fused_computation.26 | loop fusion | bytes 3932160 | tf_op jit(solution)/shard_map/stack | solution.py:63
  41.7 1.0 copy.16
  42.7 0.9 constant_dynamic-update-slice_fusion.16
  43.6 2.1 %copy.17 = bf16[1,2,8,30,128]{4,2,3,1,0:T(8,128)(2,1)} copy(bf16[1,2,8,30,128]{3,2,4,1,0:T(8,128)(2,1)} %get-tuple-element.23) | data formatting | bytes 245760 | tf_op jit(solution)/shard_map/stack | solution.py:63
  45.6 2.1 %copy.18 = bf16[1,2,8,30,128]{4,2,3,1,0:T(8,128)(2,1)} copy(bf16[1,2,8,30,128]{3,2,4,1,0:T(8,128)(2,1)} %get-tuple-element.22) | data formatting | bytes 245760 | tf_op jit(solution)/shard_map/stack | solution.py:63
  47.7 2.1 %copy.19 = bf16[1,2,8,30,128]{4,2,3,1,0:T(8,128)(2,1)} copy(bf16[1,2,8,30,128]{3,2,4,1,0:T(8,128)(2,1)} %get-tuple-element.21) | data formatting | bytes 245760 | tf_op jit(solution)/shard_map/stack | solution.py:63
  49.8 2.1 %copy.20 = bf16[1,2,8,30,128]{4,2,3,1,0:T(8,128)(2,1)} copy(bf16[1,2,8,30,128]{3,2,4,1,0:T(8,128)(2,1)} %get-tuple-element.20) | data formatting | bytes 245760 | tf_op jit(solution)/shard_map/stack | solution.py:63
  51.8 2.1 %copy.21 = bf16[1,2,8,30,128]{4,2,3,1,0:T(8,128)(2,1)} copy(bf16[1,2,8,30,128]{3,2,4,1,0:T(8,128)(2,1)} %get-tuple-element.19) | data formatting | bytes 245760 | tf_op jit(solution)/shard_map/stack | solution.py:63
  53.9 2.1 %copy.22 = bf16[1,2,8,30,128]{4,2,3,1,0:T(8,128)(2,1)} copy(bf16[1,2,8,30,128]{3,2,4,1,0:T(8,128)(2,1)} %get-tuple-element.18) | data formatting | bytes 245760 | tf_op jit(solution)/shard_map/stack | solution.py:63
  56.0 2.1 %copy.23 = bf16[1,2,8,30,128]{4,2,3,1,0:T(8,128)(2,1)} copy(bf16[1,2,8,30,128]{3,2,4,1,0:T(8,128)(2,1)} %get-tuple-element.17) | data formatting | bytes 245760 | tf_op jit(solution)/shard_map/stack | solution.py:63
  58.0 2.0 %copy.24 = bf16[1,2,8,30,128]{4,2,3,1,0:T(8,128)(2,1)} copy(bf16[1,2,8,30,128]{3,2,4,1,0:T(8,128)(2,1)} %get-tuple-element.16) | data formatting | bytes 245760 | tf_op jit(solution)/shard_map/stack | solution.py:63
  60.1 2.1 %copy.25 = bf16[1,2,8,30,128]{4,2,3,1,0:T(8,128)(2,1)} copy(bf16[1,2,8,30,128]{3,2,4,1,0:T(8,128)(2,1)} %get-tuple-element.15) | data formatting | bytes 245760 | tf_op jit(solution)/shard_map/stack | solution.py:63
  62.1 2.1 %copy.26 = bf16[1,2,8,30,128]{4,2,3,1,0:T(8,128)(2,1)} copy(bf16[1,2,8,30,128]{3,2,4,1,0:T(8,128)(2,1)} %get-tuple-element.14) | data formatting | bytes 245760 | tf_op jit(solution)/shard_map/stack | solution.py:63
  64.2 2.1 %copy.27 = bf16[1,2,8,30,128]{4,2,3,1,0:T(8,128)(2,1)} copy(bf16[1,2,8,30,128]{3,2,4,1,0:T(8,128)(2,1)} %get-tuple-element.13) | data formatting | bytes 245760 | tf_op jit(solution)/shard_map/stack | solution.py:63
  66.3 2.1 %copy.28 = bf16[1,2,8,30,128]{4,2,3,1,0:T(8,128)(2,1)} copy(bf16[1,2,8,30,128]{3,2,4,1,0:T(8,128)(2,1)} %get-tuple-element.12) | data formatting | bytes 245760 | tf_op jit(solution)/shard_map/stack | solution.py:63
  68.3 1.0 copy.29
  70.1 0.9 constant_dynamic-update-slice_fusion.15
  71.0 0.9 constant_dynamic-update-slice_fusion.14
  72.0 0.9 constant_dynamic-update-slice_fusion.13
  72.9 0.9 constant_dynamic-update-slice_fusion.12
  73.8 0.9 constant_dynamic-update-slice_fusion.11
  74.7 0.9 constant_dynamic-update-slice_fusion.10
  75.6 0.9 constant_dynamic-update-slice_fusion.9
  76.6 0.9 constant_dynamic-update-slice_fusion.8
  77.7 54.0 %all_to_all.23 = bf16[16,2,8,30,128]{4,2,3,1,0:T(8,128)(2,1)S(1)} all-to-all(bf16[16,2,8,30,128]{4,2,3,1,0:T(8,128)(2,1)S(1)} %constant_dynamic-update-slice_fusion.1), channel_id=1, replica_groups=mesh['tm'=16,'rows'=2] {'tm'}, dimensions={0} | all-to-all | bytes 3932160 | tf_op jit(solution)/shard_map/all_to_all | solution.py:63
  132.4 0.7 fusion.24
  133.1 0.9 add_convert_fusion.2
  134.7 0.7 fusion.19
  135.4 1.1 add_convert_fusion.1
  137.1 0.7 fusion.14
  137.8 1.0 add_convert_fusion
  138.7 49.4 %all_to_all.24 = bf16[32,8,30,128]{3,1,2,0:T(8,128)(2,1)S(1)} all-to-all(bf16[32,8,30,128]{3,1,2,0:T(8,128)(2,1)S(1)} %add_convert_fusion), channel_id=1, replica_groups=mesh['tm'=16,'rows'=2] {'tm'}, dimensions={0} | all-to-all | bytes 3932160 | tf_op jit(solution)/shard_map/all_to_all | solution.py:69
  188.2 1.5 copy.33
  (39 shorter events, 5.8 us)
Async XLA Ops:
  0.0 13.6 %copy-start = (bf16[2,8,480,128]{3,2,1,0:T(8,128)(2,1)S(1)}, bf16[2,8,480,128]{3,2,1,0:T(8,128)(2,1)}, u32[]{:S(2)}) copy-start(bf16[2,8,480,128]{3,2,1,0:T(8,128)(2,1)} %param.5) | copy-start | bytes 5898244
  1.2 8.6 %collective-permute-start = (bf16[2,1,480,128]{3,2,1,0:T(8,128)(2,1)S(1)}, bf16[2,1,480,128]{3,2,1,0:T(8,128)(2,1)S(1)}, u32[]{:S(2)}, u32[]{:S(2)}) collective-permute-start(bf16[2,1,480,128]{3,2,1,0:T(8,128)(2,1)S(1)} %get-tuple-element.25), channel_id=1, source_target_pairs={{0,1},{2,3},{4,5},{6,7},{8,9},{10,11},{12,13},{14,15},{16,17},{18,... | collective-permute-start | bytes 737288 | tf_op jit(solution)/shard_map/ppermute | solution.py:16
  5.2 8.4 %collective-permute-start.1 = (bf16[2,1,480,128]{3,2,1,0:T(8,128)(2,1)S(1)}, bf16[2,1,480,128]{3,2,1,0:T(8,128)(2,1)S(1)}, u32[]{:S(2)}, u32[]{:S(2)}) collective-permute-start(bf16[2,1,480,128]{3,2,1,0:T(8,128)(2,1)S(1)} %get-tuple-element.26), channel_id=1, source_target_pairs={{1,0},{3,2},{5,4},{7,6},{9,8},{11,10},{13,12},{15,14},{17,16},{19,... | collective-permute-start | bytes 737288 | tf_op jit(solution)/shard_map/ppermute | solution.py:17
  33.6 2.5 %copy-start.7 = (f32[128]{0:T(128)S(1)}, f32[128]{0:T(128)}, u32[]{:S(2)}) copy-start(f32[128]{0:T(128)} %param.8) | copy-start | bytes 1540
  33.6 2.5 %copy-start.8 = (f32[128]{0:T(128)S(1)}, f32[128]{0:T(128)}, u32[]{:S(2)}) copy-start(f32[128]{0:T(128)} %param.7) | copy-start | bytes 1540
  69.3 8.3 %copy-start.2 = (bf16[1,2,8,30,128]{4,2,3,1,0:T(8,128)(2,1)S(1)}, bf16[1,2,8,30,128]{4,2,3,1,0:T(8,128)(2,1)}, u32[]{:S(2)}) copy-start(bf16[1,2,8,30,128]{4,2,3,1,0:T(8,128)(2,1)} %copy.28) | copy-start | bytes 368644
  69.3 8.3 %copy-start.1 = (bf16[1,2,8,30,128]{4,2,3,1,0:T(8,128)(2,1)S(1)}, bf16[1,2,8,30,128]{4,2,3,1,0:T(8,128)(2,1)}, u32[]{:S(2)}) copy-start(bf16[1,2,8,30,128]{4,2,3,1,0:T(8,128)(2,1)} %copy.29) | copy-start | bytes 368644
  69.7 7.8 %copy-start.5 = (bf16[1,2,8,30,128]{4,2,3,1,0:T(8,128)(2,1)S(1)}, bf16[1,2,8,30,128]{4,2,3,1,0:T(8,128)(2,1)}, u32[]{:S(2)}) copy-start(bf16[1,2,8,30,128]{4,2,3,1,0:T(8,128)(2,1)} %copy.25) | copy-start | bytes 368644
  69.7 7.8 %copy-start.4 = (bf16[1,2,8,30,128]{4,2,3,1,0:T(8,128)(2,1)S(1)}, bf16[1,2,8,30,128]{4,2,3,1,0:T(8,128)(2,1)}, u32[]{:S(2)}) copy-start(bf16[1,2,8,30,128]{4,2,3,1,0:T(8,128)(2,1)} %copy.26) | copy-start | bytes 368644
  69.7 7.8 %copy-start.3 = (bf16[1,2,8,30,128]{4,2,3,1,0:T(8,128)(2,1)S(1)}, bf16[1,2,8,30,128]{4,2,3,1,0:T(8,128)(2,1)}, u32[]{:S(2)}) copy-start(bf16[1,2,8,30,128]{4,2,3,1,0:T(8,128)(2,1)} %copy.27) | copy-start | bytes 368644
  77.6 54.1 %copy-start.6 = (bf16[3,3,128,128]{3,2,1,0:T(8,128)(2,1)S(1)}, bf16[3,3,128,128]{3,2,1,0:T(8,128)(2,1)}, u32[]{:S(2)}) copy-start(bf16[3,3,128,128]{3,2,1,0:T(8,128)(2,1)} %param.9) | copy-start | bytes 884740
